TPU v7x, 32 devices: a whole 2x2x4 slice. The times are simulated.
32 devices in a mesh: tm: 8 (over z, y), rows: 4 (over x, core).
Axes of the slice: x: 2, y: 2, z: 4, core: 2. Of those that a mesh axis runs over, the one named last changes fastest.
Arguments:
- phases: bfloat16 [16, 512, 512], P('tm', 'rows'), may hold values from -6 to 6
- focal_data: bfloat16 [16, 2, 256, 256], P('tm', None, 'rows'), may hold values from -6 to 6
- shifts: int32 [16, 2], P('tm'), may hold values from 0 to 2, as said below
- pupil_mask: int32 [512, 512], P('rows'), may hold values 0 or 1
Outputs:
- adjoint_field: float32 [16, 512, 512], P('tm', 'rows')
- wind_grad: float32 [2], replicated
Inputs may be any that keep to these rules, and one draw needn't show every extreme that they name: `shifts`: column 0 is a frame's shift along pupil rows, 0 or 1, and sums over all frames to exactly 8; column 1 is its shift along pupil columns, 0 to 2.
All inputs are finite; a program needn't handle non-finite values. No bound on the sum of `pupil_mask` on one device may be relied on, other than what follows from the above.
Results may differ from a plain program's by a relative error of at most 0.0054.
Values may be sent and summed in bfloat16 or wider, within the bound.
No kernel may reach another device: no remote copies, remote signals or barrier semaphores. Data moves between devices by JAX's collectives and lax.ppermute only.
A program may use at most 128 MiB of HBM per device.

v0:
```python
import math
import jax
import jax.numpy as jnp
from jax import lax
from jax.sharding import PartitionSpec as P

PUPIL = 512
FOCAL = 256
decay_rate = 0.999


def from_behind(value, axis, steps):
    count = lax.axis_size(axis)
    first, last = (max(0, -steps), min(count, count - steps))
    return lax.ppermute(value, axis, [(source, source + steps) for source in range(first, last)])


def carried_in(part, axis, combine, identity):
    count = lax.axis_size(axis)
    place = lax.axis_index(axis)
    ahead = count - 1 - place
    gathered = jax.tree.map(lambda a: lax.all_gather(a, axis), part)
    state = jax.tree.map(lambda a, e: jnp.zeros_like(a) + jnp.asarray(e, a.dtype), part, identity)

    def one(step, state):
        source = count - 1 - step
        return combine(
            state, jax.tree.map(lambda a: lax.dynamic_index_in_dim(a, source, 0, False), gathered)
        )

    return lax.fori_loop(0, ahead, one, state)


def tables(row_total):
    focal_pos = jnp.arange(FOCAL, dtype=jnp.int32) - FOCAL // 2
    pupil_pos = jnp.arange(row_total, dtype=jnp.int32) - PUPIL // 2
    turns = jnp.mod(focal_pos[:, None] * pupil_pos[None, :], 2 * PUPIL)
    angle = turns.astype(jnp.float32) * (math.pi / PUPIL)
    factor = 1.0 / math.sqrt(PUPIL)
    return (
        (jnp.cos(angle) * factor).astype(jnp.bfloat16),
        (-jnp.sin(angle) * factor).astype(jnp.bfloat16),
    )


def shift_back(field_in, shift_rows, shift_cols, pad_rows):
    cols_total = field_in.shape[1]
    padded = jnp.pad(field_in, ((0, pad_rows), (0, 0)))
    start_row = jnp.minimum(shift_rows, pad_rows).astype(jnp.int32)
    moved = lax.dynamic_slice(padded, (start_row, jnp.zeros((), jnp.int32)), field_in.shape)
    start_col = jnp.minimum(shift_cols, cols_total).astype(jnp.int32)
    rolled = jnp.roll(moved, -start_col, axis=1)
    keep = jnp.arange(cols_total, dtype=jnp.int32) < cols_total - start_col
    return jnp.where(keep[None, :], rolled, jnp.zeros_like(rolled))


def adjoint_rows(cos_part, sin_part, resid, cos_full, sin_full, live):
    real_part = resid[:, 0]
    imag_part = resid[:, 1]
    w_real = (
        jnp.einsum("qn,kqs->kns", cos_part, real_part, preferred_element_type=jnp.float32)
        + jnp.einsum("qn,kqs->kns", sin_part, imag_part, preferred_element_type=jnp.float32)
    ).astype(jnp.bfloat16)
    w_imag = (
        jnp.einsum("qn,kqs->kns", cos_part, imag_part, preferred_element_type=jnp.float32)
        - jnp.einsum("qn,kqs->kns", sin_part, real_part, preferred_element_type=jnp.float32)
    ).astype(jnp.bfloat16)
    summed = jnp.einsum(
        "kns,sp->knp", w_real, cos_full, preferred_element_type=jnp.float32
    ) + jnp.einsum("kns,sp->knp", w_imag, sin_full, preferred_element_type=jnp.float32)
    return jnp.where(live[None], summed, jnp.zeros_like(summed))


def on_device(phases, focal_data, shifts, pupil_mask):
    frame_count = phases.shape[0]
    block = phases.shape[1]
    width = phases.shape[2]
    halo_rows = width // (4 * lax.axis_size("rows"))
    window = block + halo_rows
    frames_all = frame_count * lax.axis_size("tm")
    row_start = lax.axis_index("rows") * block
    cos_t, sin_t = tables(width)
    cos_rows = lax.dynamic_slice_in_dim(cos_t, row_start, block, 1)
    sin_rows = lax.dynamic_slice_in_dim(sin_t, row_start, block, 1)
    live = pupil_mask == 1
    masked = jnp.where(live[None], phases, jnp.zeros_like(phases))
    y_real = jnp.einsum("kbp,qp->kbq", masked, cos_t, preferred_element_type=jnp.float32).astype(
        jnp.bfloat16
    )
    y_imag = jnp.einsum("kbp,qp->kbq", masked, sin_t, preferred_element_type=jnp.float32).astype(
        jnp.bfloat16
    )
    e_real = jnp.einsum(
        "qb,kbs->kqs", cos_rows, y_real, preferred_element_type=jnp.float32
    ) - jnp.einsum("qb,kbs->kqs", sin_rows, y_imag, preferred_element_type=jnp.float32)
    e_imag = jnp.einsum(
        "qb,kbs->kqs", cos_rows, y_imag, preferred_element_type=jnp.float32
    ) + jnp.einsum("qb,kbs->kqs", sin_rows, y_real, preferred_element_type=jnp.float32)
    partial_field = jnp.stack([e_real, e_imag], axis=1)
    placed = lax.dynamic_update_slice_in_dim(
        jnp.zeros_like(partial_field),
        focal_data.astype(jnp.float32),
        lax.axis_index("rows") * focal_data.shape[2],
        2,
    )
    total = lax.psum(partial_field - placed, "rows")
    resid = (-total).astype(jnp.bfloat16)
    grad = adjoint_rows(cos_rows, sin_rows, resid, cos_t, sin_t, live)
    outgoing = jnp.concatenate([grad[:, :halo_rows], phases[:, :1].astype(jnp.float32)], axis=1)
    incoming = from_behind(outgoing, "rows", -1)
    grad_window = jnp.concatenate([grad, incoming[:, :halo_rows]], axis=1)
    next_phase = incoming[:, halo_rows]
    lam_next = jnp.zeros((window, width), jnp.float32)
    local_lams = [lam_next] * frame_count
    for frame in reversed(range(frame_count)):
        lam_next = grad_window[frame] + decay_rate * shift_back(
            lam_next, shifts[frame, 0], shifts[frame, 1], halo_rows
        )
        local_lams[frame] = lam_next

    def compose(earlier, later):
        field_late, rows_late, cols_late = earlier
        field_early, rows_early, cols_early = later
        moved = shift_back(field_late, rows_early, cols_early, halo_rows)
        return (field_early + moved, rows_early + rows_late, cols_early + cols_late)

    time_index = lax.axis_index("tm").astype(jnp.float32)
    frames_float = jnp.float32(frame_count)
    start_weight = jnp.power(jnp.float32(decay_rate), time_index * frames_float)
    after_weight = jnp.power(jnp.float32(decay_rate), (time_index + 1.0) * frames_float)
    segment = (start_weight * local_lams[0], jnp.sum(shifts[:, 0]), jnp.sum(shifts[:, 1]))
    identity = (
        jnp.zeros((window, width), jnp.float32),
        jnp.zeros((), jnp.int32),
        jnp.zeros((), jnp.int32),
    )
    carried = carried_in(segment, "tm", compose, identity)
    carry_field = carried[0] / after_weight
    cum_rows = jnp.zeros((), jnp.int32)
    cum_cols = jnp.zeros((), jnp.int32)
    factor_now = 1.0
    results = [None] * frame_count
    wind_terms = jnp.zeros((2,), jnp.float32)
    for frame in reversed(range(frame_count)):
        cum_rows = cum_rows + shifts[frame, 0]
        cum_cols = cum_cols + shifts[frame, 1]
        factor_now = factor_now * decay_rate
        lam_now = (
            local_lams[frame][:block]
            + factor_now * shift_back(carry_field, cum_rows, cum_cols, halo_rows)[:block]
        )
        results[frame] = lam_now
        prior = lam_now - grad[frame]
        phase_wide = phases[frame].astype(jnp.float32)
        down_diff = jnp.concatenate([phase_wide[1:], next_phase[frame][None]], axis=0) - phase_wide
        side_diff = (
            jnp.concatenate([phase_wide[:, 1:], jnp.zeros((block, 1), jnp.float32)], axis=1)
            - phase_wide
        )
        wind_terms = wind_terms + jnp.stack(
            [jnp.sum(prior * down_diff), jnp.sum(prior * side_diff)]
        )
    wind_total = lax.psum(wind_terms, ("tm", "rows"))
    wind_grad = -wind_total / (width * frames_all)
    return (jnp.stack(results), wind_grad)


def solution(mesh):
    in_specs = (P("tm", "rows", None), P("tm", None, "rows", None), P("tm", None), P("rows", None))
    out_specs = (P("tm", "rows", None), P())
    return jax.shard_map(
        on_device, mesh=mesh, in_specs=in_specs, out_specs=out_specs, check_vma=False
    )
```

profile of v0, /device:TPU:10, one launch (start us, length us, event | category | flops | bytes accessed | tf_op | source)
XLA Modules:
  0.0 205.0 jit_solution(5280239042535664271)
XLA Ops:
  7.2 1.0 broadcast_compare_fusion
  8.2 2.5 %multiply_convert_fusion = (bf16[256,512]{1,0:T(8,128)(2,1)S(1)}, bf16[256,512]{1,0:T(8,128)(2,1)S(1)}) fusion(s32[512]{0:T(512)S(1)} %iota_add_fusion, s32[256]{0:T(256)S(1)} %iota_add_fusion.1), kind=kLoop, calls=%fused_computation.43 | loop fusion | flops 2490368 | bytes 527360 | tf_op jit(solution)/shard_map/convert_element_type | solution.py:42
  10.7 3.3 %convolution_convert_fusion = bf16[2,128,256]{2,1,0:T(8,128)(2,1)S(1)} fusion(bf16[2,128,512]{2,1,0:T(8,128)(2,1)} %param.8, pred[128,512]{1,0:T(8,128)(4,1)S(1)} %broadcast_compare_fusion, s32[512]{0:T(512)S(1)} %iota_add_fusion, s32[256]{0:T(256)S(1)} %iota_add_fusion.1), kind=kOutput, calls=%fused_computation.17 | convolution fusion | flops 69533696 | bytes 461824 | tf_op jit(solution)/shard_map/kbp,qp->kbq/dot_general | solution.py:90
  14.0 2.2 %convolution_convert_fusion.1 = bf16[2,128,256]{2,1,0:T(8,128)(2,1)S(1)} fusion(bf16[2,128,512]{2,1,0:T(8,128)(2,1)S(1)} %copy-done, pred[128,512]{1,0:T(8,128)(4,1)S(1)} %broadcast_compare_fusion, s32[512]{0:T(512)S(1)} %iota_add_fusion, s32[256]{0:T(256)S(1)} %iota_add_fusion.1), kind=kOutput, calls=%fused_computation.18 | convolution fusion | flops 69402624 | bytes 461824 | tf_op jit(solution)/shard_map/kbp,qp->kbq/dot_general | solution.py:87
  16.2 0.2 fusion.55
  16.5 0.2 fusion.57
  16.7 0.3 fusion.3
  17.0 0.3 fusion.4
  17.5 1.4 dynamic_update_slice.3
  18.9 1.2 maximum_subtract_fusion
  20.1 0.6 fusion.104
  23.2 34.5 %all-reduce.11.cloned.1.call-done = f32[2,2,256,256]{2,3,0,1:T(8,128)} async-done(((f32[2,2,256,256]{2,3,0,1:T(8,128)}), f32[2,2,256,256]{2,3,0,1:T(8,128)}) %all-reduce.11.cloned.1.call-update) | async-done | bytes 1048592 | tf_op jit(solution)/shard_map/psum | solution.py:106
  57.7 1.3 negate_convert_fusion
  59.0 0.2 fusion.43
  59.3 0.2 fusion.44
  59.5 2.2 %fusion.10 = f32[2,128,512]{2,1,0:T(8,128)S(1)} fusion(f32[2,256,128]{1,2,0:T(8,128)S(1)} %fusion.43, bf16[2,2,256,256]{2,3,0,1:T(8,128)(2,1)S(1)} %negate_convert_fusion, s32[512]{0:T(512)S(1)} %iota_add_fusion, s32[256]{0:T(256)S(1)} %iota_add_fusion.1, bf16[256,512]{1,0:T(8,128)(2,1)S(1)} %get-tuple-element.162, s32[]{:T(128)S(6)} %select_n.122), kind=kOutput, calls=%fused_computation.21 | convolution fusion | flops 102891520 | bytes 1117188 | tf_op jit(solution)/shard_map/kns,sp->knp/dot_general | solution.py:68
  61.7 3.1 %fusion.5 = f32[2,128,512]{2,1,0:T(8,128)S(1)} fusion(f32[2,128,512]{2,1,0:T(8,128)S(1)} %fusion.10, f32[2,256,128]{1,2,0:T(8,128)S(1)} %fusion.44, pred[128,512]{1,0:T(8,128)(4,1)S(1)} %broadcast_compare_fusion, bf16[2,2,256,256]{2,3,0,1:T(8,128)(2,1)S(1)} %negate_convert_fusion, s32[512]{0:T(512)S(1)} %iota_add_fusion, s32[256]{0:T(256)S(1)} %iota_add_fusion.1, ...), kind=kOutput, calls=%fused_computation.12 | convolution fusion | flops 103284736 | bytes 1707012 | tf_op jit(solution)/shard_map/kns,sp->knp/dot_general | solution.py:70
  64.8 2.1 %collective-permute-start = (f32[2,33,512]{2,1,0:T(8,128)S(1)}, f32[2,33,512]{2,1,0:T(8,128)S(1)}, u32[]{:S(2)}, u32[]{:S(2)}) collective-permute-start(f32[2,33,512]{2,1,0:T(8,128)S(1)} %pad_maximum_fusion.2), channel_id=1, source_target_pairs={{1,0},{2,1},{3,2},{5,4},{6,5},{7,6},{9,8},{10,9},{11,10},{13,12},{... | collective-permute-start | bytes 405512 | tf_op jit(solution)/shard_map/ppermute | solution.py:15
  68.4 1.2 collective-permute-done
  69.6 0.2 fusion.21
  69.9 1.0 broadcast_multiply_fusion
  70.9 0.6 dynamic-slice
  71.5 0.8 slice_reduce_fusion
  72.3 1.4 dynamic-update-slice
  73.6 1.3 dynamic-update-slice.1
  75.0 10.4 %all-reduce.8 = (s32[8]{0:T(128)S(1)}, s32[8]{0:T(128)S(1)}) all-reduce(s32[8]{0:T(128)S(1)} %dynamic-update-slice, s32[8]{0:T(128)S(1)} %dynamic-update-slice.1), channel_id=1, replica_groups=mesh['tm'=8,'rows'=4] {'tm'}, use_global_device_ids=true, to_apply=%add.6 | all-reduce | flops 16 | bytes 128
  87.2 39.7 %all-gather.3.cloned.1.call-done = f32[1280,512]{1,0:T(8,128)} async-done(((f32[160,512]{1,0:T(8,128)}), f32[1280,512]{1,0:T(8,128)}) %all-gather.3.cloned.1.call-update) | async-done | bytes 2621456 | tf_op jit(solution)/shard_map/all_gather | solution.py:22
  126.9 19.4 %while.16 = (s32[]{:T(128)}, f32[160,512]{1,0:T(8,128)S(1)}, s32[]{:T(128)}, f32[8,160,512]{2,1,0:T(8,128)}, s32[8]{0:T(128)S(1)}, /*index=5*/s32[8]{0:T(128)S(1...) while((s32[]{:T(128)}, f32[160,512]{1,0:T(8,128)S(1)}, ...), condition=%wide.region_4.6_spmd, body=%wide.region_3.5_spmd.sunk | while | flops 246299 | bytes 1639884 | solution.py:31
  126.9 0.6 dynamic_slice.173
  128.1 0.7 dynamic_slice.174
  129.5 1.2 fusion.110
  130.8 0.6 dynamic_slice.173
  132.0 0.7 dynamic_slice.174
  133.4 1.2 fusion.110
  134.6 0.6 dynamic_slice.173
  135.9 0.7 dynamic_slice.174
  137.3 1.2 fusion.110
  138.5 0.6 dynamic_slice.173
  139.8 0.7 dynamic_slice.174
  141.1 1.2 fusion.110
  142.4 0.6 dynamic_slice.173
  143.7 0.7 dynamic_slice.174
  145.0 1.2 fusion.110
  146.4 1.1 fusion.38
  147.5 2.6 %maximum_add_fusion = f32[2]{0:T(128)S(1)} fusion(f32[1]{0:T(128)} %bitcast.37, f32[1]{0:T(128)} %bitcast.36, f32[1]{0:T(128)} %bitcast.43, f32[1]{0:T(128)} %bitcast.42), kind=kLoop, calls=%fused_computation.140 | loop fusion | flops 6 | bytes 24 | tf_op jit(solution)/shard_map/add | solution.py:160
  150.1 46.7 %psum.15 = f32[2]{0:T(128)S(1)} all-reduce(f32[2]{0:T(128)S(1)} %maximum_add_fusion), channel_id=1, replica_groups=mesh['tm'=8,'rows'=4] {'tm','rows'}, use_global_device_ids=true, to_apply=%region_9.11 | all-reduce | flops 2 | bytes 16 | tf_op jit(solution)/shard_map/psum | solution.py:163
  196.9 0.5 negate_multiply_fusion
  197.4 0.8 pad_maximum_fusion
  (46 shorter events, 1.3 us)
Async XLA Ops:
  7.2 6.8 %copy-start = (bf16[2,128,512]{2,1,0:T(8,128)(2,1)S(1)}, bf16[2,128,512]{2,1,0:T(8,128)(2,1)}, u32[]{:S(2)}) copy-start(bf16[2,128,512]{2,1,0:T(8,128)(2,1)} %param.8) | copy-start | bytes 786436
  7.2 50.5 %all-reduce.11.cloned.1.call-start = ((), (), s32[]{:S(2)}) async-start(), calls=%async_computation | async-start | bytes 2097152 | tf_op jit(solution)/shard_map/psum | solution.py:106
  10.7 48.8 %copy-start.1 = (bf16[256,512]{1,0:T(8,128)(2,1)}, bf16[256,512]{1,0:T(8,128)(2,1)S(1)}, u32[]{:S(2)}) copy-start(bf16[256,512]{1,0:T(8,128)(2,1)S(1)} %get-tuple-element.162) | copy-start | bytes 786436
  16.2 1.1 copy-start.2
  17.5 2.6 %copy-start.3 = (s32[2,2]{1,0:T(2,128)S(1)}, s32[2,2]{1,0:T(2,128)}, u32[]{:S(2)}) copy-start(s32[2,2]{1,0:T(2,128)} %param.10) | copy-start | bytes 52
  20.1 106.8 %all-gather.3.cloned.1.call-start = ((), (), s32[]{:S(2)}) async-start(), calls=%async_computation.1 | async-start | bytes 2949120 | tf_op jit(solution)/shard_map/all_gather | solution.py:22
  64.8 4.7 %collective-permute-start = (f32[2,33,512]{2,1,0:T(8,128)S(1)}, f32[2,33,512]{2,1,0:T(8,128)S(1)}, u32[]{:S(2)}, u32[]{:S(2)}) collective-permute-start(f32[2,33,512]{2,1,0:T(8,128)S(1)} %pad_maximum_fusion.2), channel_id=1, source_target_pairs={{1,0},{2,1},{3,2},{5,4},{6,5},{7,6},{9,8},{10,9},{11,10},{13,12},{... | collective-permute-start | bytes 405512 | tf_op jit(solution)/shard_map/ppermute | solution.py:15
  67.0 3.9 %copy-start.4 = (u32[32]{0:T(128)S(1)}, u32[32]{0:T(128)}, u32[]{:S(2)}) copy-start(u32[32]{0:T(128)} %constant.215) | copy-start | bytes 388
Sparse Core Ops, SparseCore 0:
  20.2 37.4 all-reduce.10
  71.0 55.8 all-gather.2
where the time goes:
time: 206 us; the launch traced here: 205 us
  waiting for transfers between devices  75.4 us (37%)
  blocking collectives  57.1 us (28%)
  between operations  19.6 us (10%)
  other arithmetic  19.3 us (9%)
  local copies, waits for them, and re-layouts  12.5 us (6%)
  matrix products  12.2 us (6%)
  loops' own time  6.83 us (3%)
  starting transfers between devices  2.18 us (1%)
    psum x1, blocking collectives, on_device(): wind_total = lax.psum(wind_terms, ('tm', 'rows'))  46.7 us
    all_gather x1, waiting for transfers between devices, carried_in(): gathered = jax.tree.map(lambda a: lax.all_gather(a, axis), part)  39.7 us
    psum x1, waiting for transfers between devices, on_device(): total = lax.psum(partial_field - placed, 'rows')  34.5 us
    unnamed x1, blocking collectives  10.4 us
    another operation x1, loops' own time, carried_in(): return lax.fori_loop(0, ahead, one, state)  6.83 us
    dynamic_slice x10, local copies, waits for them, and re-layouts, one(): lax.dynamic_index_in_dim(a, source, 0, False)  6.21 us
    add x5, other arithmetic, compose(): return (field_early + moved, rows_early + rows_late, cols_early + cols_late)  6.12 us
  transfers between devices with their start and end apart: 3, of which 3 were waited for; matrix products, arithmetic and copies ran while one was open for 3% of the time, Pallas kernels for 0%

commit v1 on v0

--- a/solution.py
+++ b/solution.py
@@ -103,7 +103,9 @@
         lax.axis_index("rows") * focal_data.shape[2],
         2,
     )
-    total = lax.psum(partial_field - placed, "rows")
+    part_2 = partial_field - placed
+    blocks = lax.all_gather(part_2, "rows")
+    total = jnp.sum(blocks, axis=0)
     resid = (-total).astype(jnp.bfloat16)
     grad = adjoint_rows(cos_rows, sin_rows, resid, cos_t, sin_t, live)
     outgoing = jnp.concatenate([grad[:, :halo_rows], phases[:, :1].astype(jnp.float32)], axis=1)

time: 206 us -> 205 us (level)
  waiting for transfers between devices: 75.4 us -> 73 us
    psum x1 -> x0, waiting for transfers between devices: 34.5 us -> none  [on_device(): total = lax.psum(partial_field - placed, 'rows')]
    all_gather x0 -> x1, waiting for transfers between devices: none -> 31.9 us  [on_device(): blocks = lax.all_gather(part_2, 'rows')]
    reduce_sum x0 -> x1, other arithmetic: none -> 2.6 us  [on_device(): total = jnp.sum(blocks, axis=0)]
where the time goes in v1:
time: 205 us; the launch traced here: 204 us
  waiting for transfers between devices  73 us (36%)
  blocking collectives  56.9 us (28%)
  other arithmetic  20.6 us (10%)
  between operations  19.7 us (10%)
  matrix products  12.2 us (6%)
  local copies, waits for them, and re-layouts  12.1 us (6%)
  loops' own time  6.46 us (3%)
  starting transfers between devices  3.49 us (2%)
    psum x1, blocking collectives, on_device(): wind_total = lax.psum(wind_terms, ('tm', 'rows'))  46.4 us
    all_gather x1, waiting for transfers between devices, carried_in(): gathered = jax.tree.map(lambda a: lax.all_gather(a, axis), part)  39.8 us
    all_gather x1, waiting for transfers between devices, on_device(): blocks = lax.all_gather(part_2, 'rows')  31.9 us
    unnamed x1, blocking collectives  10.4 us
    another operation x1, loops' own time, carried_in(): return lax.fori_loop(0, ahead, one, state)  6.46 us
    add x5, other arithmetic, compose(): return (field_early + moved, rows_early + rows_late, cols_early + cols_late)  6.12 us
    dynamic_slice x10, local copies, waits for them, and re-layouts, one(): lax.dynamic_index_in_dim(a, source, 0, False)  5.85 us
  transfers between devices with their start and end apart: 3, of which 3 were waited for; matrix products, arithmetic and copies ran while one was open for 3% of the time, Pallas kernels for 0%

profile of v1, /device:TPU:10, one launch (start us, length us, event | category | flops | bytes accessed | tf_op | source)
XLA Modules:
  0.0 204.4 jit_solution(16034374598653330286)
XLA Ops:
  7.2 1.0 broadcast_compare_fusion
  8.2 2.5 %multiply_convert_fusion = (bf16[256,512]{1,0:T(8,128)(2,1)S(1)}, bf16[256,512]{1,0:T(8,128)(2,1)S(1)}) fusion(s32[512]{0:T(512)S(1)} %iota_add_fusion, s32[256]{0:T(256)S(1)} %iota_add_fusion.1), kind=kLoop, calls=%fused_computation.43 | loop fusion | flops 2490368 | bytes 527360 | tf_op jit(solution)/shard_map/convert_element_type | solution.py:42
  10.7 3.3 %convolution_convert_fusion = bf16[2,128,256]{2,1,0:T(8,128)(2,1)S(1)} fusion(bf16[2,128,512]{2,1,0:T(8,128)(2,1)} %param.8, pred[128,512]{1,0:T(8,128)(4,1)S(1)} %broadcast_compare_fusion, s32[512]{0:T(512)S(1)} %iota_add_fusion, s32[256]{0:T(256)S(1)} %iota_add_fusion.1), kind=kOutput, calls=%fused_computation.17 | convolution fusion | flops 69533696 | bytes 461824 | tf_op jit(solution)/shard_map/kbp,qp->kbq/dot_general | solution.py:90
  14.0 2.2 %convolution_convert_fusion.1 = bf16[2,128,256]{2,1,0:T(8,128)(2,1)S(1)} fusion(bf16[2,128,512]{2,1,0:T(8,128)(2,1)S(1)} %copy-done, pred[128,512]{1,0:T(8,128)(4,1)S(1)} %broadcast_compare_fusion, s32[512]{0:T(512)S(1)} %iota_add_fusion, s32[256]{0:T(256)S(1)} %iota_add_fusion.1), kind=kOutput, calls=%fused_computation.18 | convolution fusion | flops 69402624 | bytes 461824 | tf_op jit(solution)/shard_map/kbp,qp->kbq/dot_general | solution.py:87
  16.2 0.2 fusion.55
  16.5 0.2 fusion.57
  16.7 0.3 fusion.3
  17.0 0.3 fusion.4
  17.5 1.4 dynamic_update_slice.3
  18.9 1.1 maximum_subtract_fusion
  20.0 0.2 all-gather.7.cloned.1.call-start
  20.3 0.7 fusion.104
  23.5 31.9 %all-gather.5.cloned.1.call-done = f32[8,2,256,256]{2,3,0,1:T(8,128)} async-done(((f32[2,2,256,256]{2,3,0,1:T(8,128)}), f32[8,2,256,256]{2,3,0,1:T(8,128)}) %all-gather.5.cloned.1.call-update) | async-done | bytes 4194320 | tf_op jit(solution)/shard_map/all_gather | solution.py:107
  55.4 2.6 %reduce_sum.63 = f32[2,2,256,256]{2,3,0,1:T(8,128)S(1)} reduce(f32[4,2,2,256,256]{3,4,1,0,2:T(8,128)} %bitcast.135, f32[]{:T(128)} %constant.184.clone.1), dimensions={0}, to_apply=%region_0.1 | reduce | flops 786432 | bytes 5242884 | tf_op jit(solution)/shard_map/reduce_sum | solution.py:108
  58.3 0.2 fusion.44
  58.5 2.2 %fusion.10 = f32[2,128,512]{2,1,0:T(8,128)S(1)} fusion(f32[2,256,128]{2,1,0:T(8,128)S(1)} %fusion.43, bf16[2,2,256,256]{2,3,0,1:T(8,128)(2,1)S(1)} %negate_convert_fusion, s32[512]{0:T(512)S(1)} %iota_add_fusion, s32[256]{0:T(256)S(1)} %iota_add_fusion.1, bf16[256,512]{1,0:T(8,128)(2,1)S(1)} %get-tuple-element.162, s32[]{:T(128)S(6)} %select_n.122), kind=kOutput, calls=%fused_computation.21 | convolution fusion | flops 102891520 | bytes 1117188 | tf_op jit(solution)/shard_map/kns,sp->knp/dot_general | solution.py:68
  60.8 3.1 %fusion.5 = f32[2,128,512]{2,1,0:T(8,128)S(1)} fusion(f32[2,128,512]{2,1,0:T(8,128)S(1)} %fusion.10, f32[2,256,128]{2,1,0:T(8,128)S(1)} %fusion.44, pred[128,512]{1,0:T(8,128)(4,1)S(1)} %broadcast_compare_fusion, bf16[2,2,256,256]{2,3,0,1:T(8,128)(2,1)S(1)} %negate_convert_fusion, s32[512]{0:T(512)S(1)} %iota_add_fusion, s32[256]{0:T(256)S(1)} %iota_add_fusion.1, ...), kind=kOutput, calls=%fused_computation.12 | convolution fusion | flops 103284736 | bytes 1707012 | tf_op jit(solution)/shard_map/kns,sp->knp/dot_general | solution.py:70
  63.9 3.2 %collective-permute-start = (f32[2,33,512]{2,1,0:T(8,128)S(1)}, f32[2,33,512]{2,1,0:T(8,128)S(1)}, u32[]{:S(2)}, u32[]{:S(2)}) collective-permute-start(f32[2,33,512]{2,1,0:T(8,128)S(1)} %pad_maximum_fusion.2), channel_id=1, source_target_pairs={{1,0},{2,1},{3,2},{5,4},{6,5},{7,6},{9,8},{10,9},{11,10},{13,12},{... | collective-permute-start | bytes 405512 | tf_op jit(solution)/shard_map/ppermute | solution.py:15
  68.6 1.3 collective-permute-done
  70.0 0.2 fusion.21
  70.3 1.0 broadcast_multiply_fusion
  71.3 0.6 dynamic-slice
  71.9 0.7 slice_reduce_fusion
  72.6 1.3 dynamic-update-slice
  73.9 1.4 dynamic-update-slice.1
  75.2 10.4 %all-reduce.8 = (s32[8]{0:T(128)S(1)}, s32[8]{0:T(128)S(1)}) all-reduce(s32[8]{0:T(128)S(1)} %dynamic-update-slice, s32[8]{0:T(128)S(1)} %dynamic-update-slice.1), channel_id=1, replica_groups=mesh['tm'=8,'rows'=4] {'tm'}, use_global_device_ids=true, to_apply=%add.6 | all-reduce | flops 16 | bytes 128
  87.5 39.8 %all-gather.7.cloned.1.call-done = f32[1280,512]{1,0:T(8,128)} async-done(((f32[160,512]{1,0:T(8,128)}), f32[1280,512]{1,0:T(8,128)}) %all-gather.7.cloned.1.call-update) | async-done | bytes 2621456 | tf_op jit(solution)/shard_map/all_gather | solution.py:22
  127.3 18.6 %while.16 = (s32[]{:T(128)}, f32[160,512]{1,0:T(8,128)S(1)}, s32[]{:T(128)}, f32[8,160,512]{2,1,0:T(8,128)}, s32[8]{0:T(128)S(1)}, /*index=5*/s32[8]{0:T(128)S(1...) while((s32[]{:T(128)}, f32[160,512]{1,0:T(8,128)S(1)}, ...), condition=%wide.region_4.6_spmd, body=%wide.region_3.5_spmd.sunk | while | flops 246299 | bytes 1639884 | solution.py:31
  127.3 0.6 dynamic_slice.173
  128.5 0.6 dynamic_slice.174
  129.8 1.2 fusion.110
  131.0 0.6 dynamic_slice.173
  132.3 0.6 dynamic_slice.174
  133.5 1.2 fusion.110
  134.7 0.6 dynamic_slice.173
  136.0 0.6 dynamic_slice.174
  137.2 1.2 fusion.110
  138.5 0.6 dynamic_slice.173
  139.7 0.6 dynamic_slice.174
  140.9 1.2 fusion.110
  142.2 0.6 dynamic_slice.173
  143.5 0.6 dynamic_slice.174
  144.7 1.2 fusion.110
  146.1 1.1 fusion.38
  147.2 2.6 %maximum_add_fusion = f32[2]{0:T(128)S(1)} fusion(f32[1]{0:T(128)} %bitcast.38, f32[1]{0:T(128)} %bitcast.37, f32[1]{0:T(128)} %bitcast.44, f32[1]{0:T(128)} %bitcast.43), kind=kLoop, calls=%fused_computation.140 | loop fusion | flops 6 | bytes 24 | tf_op jit(solution)/shard_map/add | solution.py:162
  149.8 46.4 %psum.7 = f32[2]{0:T(128)S(1)} all-reduce(f32[2]{0:T(128)S(1)} %maximum_add_fusion), channel_id=1, replica_groups=mesh['tm'=8,'rows'=4] {'tm','rows'}, use_global_device_ids=true, to_apply=%region_9.11 | all-reduce | flops 2 | bytes 16 | tf_op jit(solution)/shard_map/psum | solution.py:165
  196.2 0.5 negate_multiply_fusion
  196.8 0.8 pad_maximum_fusion
  (47 shorter events, 1.6 us)
Async XLA Ops:
  7.2 6.8 %copy-start = (bf16[2,128,512]{2,1,0:T(8,128)(2,1)S(1)}, bf16[2,128,512]{2,1,0:T(8,128)(2,1)}, u32[]{:S(2)}) copy-start(bf16[2,128,512]{2,1,0:T(8,128)(2,1)} %param.8) | copy-start | bytes 786436
  7.2 48.2 %all-gather.5.cloned.1.call-start = ((), (), s32[]{:S(2)}) async-start(), calls=%async_computation | async-start | bytes 5242880 | tf_op jit(solution)/shard_map/all_gather | solution.py:107
  10.7 47.8 %copy-start.1 = (bf16[256,512]{1,0:T(8,128)(2,1)}, bf16[256,512]{1,0:T(8,128)(2,1)S(1)}, u32[]{:S(2)}) copy-start(bf16[256,512]{1,0:T(8,128)(2,1)S(1)} %get-tuple-element.162) | copy-start | bytes 786436
  16.2 1.1 copy-start.2
  17.5 2.8 %copy-start.3 = (s32[2,2]{1,0:T(2,128)S(1)}, s32[2,2]{1,0:T(2,128)}, u32[]{:S(2)}) copy-start(s32[2,2]{1,0:T(2,128)} %param.10) | copy-start | bytes 52
  20.0 107.2 %all-gather.7.cloned.1.call-start = ((), (), s32[]{:S(2)}) async-start(), calls=%async_computation.1 | async-start | bytes 2949120 | tf_op jit(solution)/shard_map/all_gather | solution.py:22
  63.9 6.1 %collective-permute-start = (f32[2,33,512]{2,1,0:T(8,128)S(1)}, f32[2,33,512]{2,1,0:T(8,128)S(1)}, u32[]{:S(2)}, u32[]{:S(2)}) collective-permute-start(f32[2,33,512]{2,1,0:T(8,128)S(1)} %pad_maximum_fusion.2), channel_id=1, source_target_pairs={{1,0},{2,1},{3,2},{5,4},{6,5},{7,6},{9,8},{10,9},{11,10},{13,12},{... | collective-permute-start | bytes 405512 | tf_op jit(solution)/shard_map/ppermute | solution.py:15
  67.2 4.1 %copy-start.4 = (u32[32]{0:T(128)S(1)}, u32[32]{0:T(128)}, u32[]{:S(2)}) copy-start(u32[32]{0:T(128)} %constant.215) | copy-start | bytes 388
Sparse Core Ops, SparseCore 0:
  20.1 35.1 all-gather.4
  71.4 55.8 all-gather.6
